TPU v7x, 512 devices: a whole 4x4x16 slice. The times are simulated.
512 devices in a mesh: space: 64 (over z, x), member: 8 (over y, core).
Axes of the slice: x: 4, y: 4, z: 16, core: 2. Of those that a mesh axis runs over, the one named last changes fastest.
Arguments:
- spectra: float32 [16, 36, 256, 720], P('member', None, 'space'), may hold values from 0.5 to 2
- group_speed: float32 [256, 720], P('space'), may hold values from 0.15 to 0.5
- turning_rate: float32 [256, 720], P('space'), may hold values from -0.28 to 0.28
- obs_cell: int32 [2, 1024], replicated, may hold values from 0 to 184319, as said below
- obs_value: float32 [2, 1024], replicated, may hold values from 0.9 to 1.6
- obs_variance: float32 [2, 1024], replicated, may hold values from 0.001 to 0.01
Outputs:
- analysis: float32 [16, 36, 184320], P(None, None, ('space', 'member'))
Inputs may be any that keep to these rules, and one draw needn't show every extreme that they name: `obs_cell`: every block of 360 consecutive cells starting at a multiple of 360 holds the cell of at least one observation in every batch.
All inputs are finite; a program needn't handle non-finite values.
Results may differ from a plain program's by a relative error of at most 0.0003.
Values sent between devices are 32-bit elements; how exact they have to be, the bound alone decides.
A program may use at most 64 MiB of HBM per device.

v0:
```python
import math
import jax
import jax.numpy as jnp
from jax import lax
from jax.sharding import PartitionSpec as P

LON = 720
STEPS = 4
BATCHES = 2
LOC = 4
HIGH = lax.Precision.HIGHEST


def padded_2(cells, sides, width):
    for axis, dim in sides:
        count = lax.axis_size(axis)
        ends = count - 1
        head = lax.slice_in_dim(cells, 0, width, axis=dim)
        tail = lax.slice_in_dim(cells, cells.shape[dim] - width, cells.shape[dim], axis=dim)
        cells = jnp.concatenate(
            [
                lax.ppermute(tail, axis, [(i, (i + 1) % count) for i in range(ends)]),
                cells,
                lax.ppermute(head, axis, [((i + 1) % count, i) for i in range(ends)]),
            ],
            axis=dim,
        )
    return cells


def copy_for_each(array, axis):
    devices = lax.axis_size(axis)
    return lax.all_to_all(
        jnp.broadcast_to(array[None], (devices, *array.shape)), axis, 0, 0, tiled=True
    )


def over_copies(array, axis):
    everything = copy_for_each(array, axis)
    return jnp.sum(everything, axis=0)


def transport(padded, speed, turning, cosines, sines):
    centre = padded[:, :, 1:-1, :]
    south = padded[:, :, :-2, :]
    north = padded[:, :, 2:, :]
    along_x = speed[None] * cosines[:, None, None]
    along_y = speed[None] * sines[:, None, None]
    along_turn = turning[None] * cosines[:, None, None]
    west = jnp.roll(centre, 1, axis=3)
    east = jnp.roll(centre, -1, axis=3)
    behind = jnp.roll(centre, 1, axis=1)
    ahead = jnp.roll(centre, -1, axis=1)
    result = (
        centre
        - jnp.maximum(along_x, 0.0) * (centre - west)
        - jnp.minimum(along_x, 0.0) * (east - centre)
    )
    result = (
        result
        - jnp.maximum(along_y, 0.0) * (centre - south)
        - jnp.minimum(along_y, 0.0) * (north - centre)
    )
    result = (
        result
        - jnp.maximum(along_turn, 0.0) * (centre - behind)
        - jnp.minimum(along_turn, 0.0) * (ahead - centre)
    )
    return result


def panel(prior, values, variance):
    members = prior.shape[1]
    centre = jnp.mean(prior, axis=1)
    anomaly = prior - centre[:, None]
    spread = jnp.sum(anomaly * anomaly, axis=1) / (members - 1)
    total = spread + variance
    shrink = 1.0 / (1.0 + jnp.sqrt(variance / total))
    weights_obs = ((values - centre)[:, None] - shrink[:, None] * anomaly) / total[:, None]
    outer = anomaly[:, :, None] * weights_obs[:, None, :]
    return outer.reshape(prior.shape[0], members * members) / (members - 1)


def taper(cell_ids, targets):
    lat_gap = cell_ids[:, None] // LON - targets[None, :] // LON
    lon_gap = jnp.abs(cell_ids[:, None] % LON - targets[None, :] % LON)
    lon_gap = jnp.minimum(lon_gap, LON - lon_gap)
    square = (lat_gap * lat_gap + lon_gap * lon_gap).astype(jnp.float32)
    near = jnp.maximum(1.0 - square / (LOC * LOC), 0.0)
    return near * near


def per_device(spectra, group_speed, turning_rate, obs_cell, obs_value, obs_variance):
    local_members, directions, rows, width = spectra.shape
    angles = 2.0 * math.pi * jnp.arange(directions, dtype=jnp.float32) / directions
    cosines = jnp.cos(angles)
    sines = jnp.sin(angles)
    energy = spectra
    for step in range(STEPS):
        padded = padded_2(energy, (("space", 2),), 1)
        energy = transport(padded, group_speed, turning_rate, cosines, sines)
    state = lax.all_to_all(
        energy.reshape(local_members, directions, rows * width),
        "member",
        split_axis=2,
        concat_axis=0,
        tiled=True,
    )
    members, directions, owned = state.shape
    first_cell = (
        lax.axis_index("space") * lax.axis_size("member") + lax.axis_index("member")
    ) * owned
    cell_ids = first_cell + jnp.arange(owned, dtype=jnp.int32)
    for batch in range(BATCHES):
        targets = obs_cell[batch]
        mean_dir = jnp.mean(state, axis=1)
        onehot = (targets[:, None] == cell_ids[None, :]).astype(jnp.float32)
        partial_prior = jnp.dot(onehot, mean_dir.T, precision=HIGH)
        slab_prior = over_copies(partial_prior, "member")
        beside_all = padded_2(slab_prior[None], (("space", 0),), 1)
        prior = jnp.sum(beside_all, axis=0)
        mixing = panel(prior, obs_value[batch], obs_variance[batch])
        gain = jnp.dot(taper(cell_ids, targets), mixing, precision=HIGH).reshape(
            owned, members, members
        )
        deviation = state - jnp.mean(state, axis=0, keepdims=True)
        state = state + jnp.einsum("kdc,ckl->ldc", deviation, gain, precision=HIGH)
    return state


def solution(mesh):
    placed = (P("member", None, "space", None), P("space", None), P("space", None), P(), P(), P())
    return jax.shard_map(
        per_device,
        mesh=mesh,
        in_specs=placed,
        out_specs=P(None, None, ("space", "member")),
        check_vma=False,
    )
```

profile of v0, /device:TPU:230, one launch (start us, length us, event | category | flops | bytes accessed | tf_op | source)
XLA Modules:
  0.0 194.1 jit_solution(2479666879118172591)
XLA Ops:
  1.4 5.0 %collective-permute-start = (f32[2,36,1,720]{3,1,2,0:T(8,128)S(1)}, f32[2,36,1,720]{3,1,2,0:T(8,128)S(1)}, u32[]{:S(2)}, u32[]{:S(2)}) collective-permute-start(f32[2,36,1,720]{3,1,2,0:T(8,128)S(1)} %get-tuple-element.51), channel_id=1, source_target_pairs={{0,8},{8,16},{16,24},{24,32},{32,40},{40,48},{48,56},{56,64},{64,7... | collective-permute-start | bytes 622088 | tf_op jit(solution)/shard_map/ppermute | solution.py:22
  11.5 7.4 %collective-permute-done.1 = f32[2,36,1,720]{3,1,2,0:T(8,128)S(1)} collective-permute-done((f32[2,36,1,720]{3,1,2,0:T(8,128)S(1)}, f32[2,36,1,720]{3,1,2,0:T(8,128)S(1)}, u32[]{:S(2)}, u32[]{:S(2)}) %collective-permute-start.1) | collective-permute-done | bytes 207392 | tf_op jit(solution)/shard_map/ppermute | solution.py:24
  22.5 3.9 %collective-permute-start.3 = (f32[2,36,1,720]{3,1,2,0:T(8,128)S(1)}, f32[2,36,1,720]{3,1,2,0:T(8,128)S(1)}, u32[]{:S(2)}, u32[]{:S(2)}) collective-permute-start(f32[2,36,1,720]{3,1,2,0:T(8,128)S(1)} %get-tuple-element.42), channel_id=1, source_target_pairs={{8,0},{16,8},{24,16},{32,24},{40,32},{48,40},{56,48},{64,56},{72,6... | collective-permute-start | bytes 622088 | tf_op jit(solution)/shard_map/ppermute | solution.py:24
  28.9 5.2 %collective-permute-done.3 = f32[2,36,1,720]{3,1,2,0:T(8,128)S(1)} collective-permute-done((f32[2,36,1,720]{3,1,2,0:T(8,128)S(1)}, f32[2,36,1,720]{3,1,2,0:T(8,128)S(1)}, u32[]{:S(2)}, u32[]{:S(2)}) %collective-permute-start.3) | collective-permute-done | bytes 207392 | tf_op jit(solution)/shard_map/ppermute | solution.py:24
  37.7 3.9 %collective-permute-start.5 = (f32[2,36,1,720]{3,1,2,0:T(8,128)S(1)}, f32[2,36,1,720]{3,1,2,0:T(8,128)S(1)}, u32[]{:S(2)}, u32[]{:S(2)}) collective-permute-start(f32[2,36,1,720]{3,1,2,0:T(8,128)S(1)} %get-tuple-element.32), channel_id=1, source_target_pairs={{8,0},{16,8},{24,16},{32,24},{40,32},{48,40},{56,48},{64,56},{72,6... | collective-permute-start | bytes 622088 | tf_op jit(solution)/shard_map/ppermute | solution.py:24
  43.8 5.2 %collective-permute-done.5 = f32[2,36,1,720]{3,1,2,0:T(8,128)S(1)} collective-permute-done((f32[2,36,1,720]{3,1,2,0:T(8,128)S(1)}, f32[2,36,1,720]{3,1,2,0:T(8,128)S(1)}, u32[]{:S(2)}, u32[]{:S(2)}) %collective-permute-start.5) | collective-permute-done | bytes 207392 | tf_op jit(solution)/shard_map/ppermute | solution.py:24
  52.6 3.9 %collective-permute-start.7 = (f32[2,36,1,720]{3,1,2,0:T(8,128)S(1)}, f32[2,36,1,720]{3,1,2,0:T(8,128)S(1)}, u32[]{:S(2)}, u32[]{:S(2)}) collective-permute-start(f32[2,36,1,720]{3,1,2,0:T(8,128)S(1)} %get-tuple-element.22), channel_id=1, source_target_pairs={{8,0},{16,8},{24,16},{32,24},{40,32},{48,40},{56,48},{64,56},{72,6... | collective-permute-start | bytes 622088 | tf_op jit(solution)/shard_map/ppermute | solution.py:24
  58.7 5.2 %collective-permute-done.7 = f32[2,36,1,720]{3,1,2,0:T(8,128)S(1)} collective-permute-done((f32[2,36,1,720]{3,1,2,0:T(8,128)S(1)}, f32[2,36,1,720]{3,1,2,0:T(8,128)S(1)}, u32[]{:S(2)}, u32[]{:S(2)}) %collective-permute-start.7) | collective-permute-done | bytes 207392 | tf_op jit(solution)/shard_map/ppermute | solution.py:24
  65.9 4.6 %copy.102 = f32[2,36,4,720]{1,0,3,2:T(2,128)S(1)} copy(f32[2,36,4,720]{3,1,2,0:T(8,128)} %fusion.52) | data formatting | bytes 1658880 | tf_op jit(solution)/shard_map/reshape | solution.py:103
  70.5 6.2 %reshape.338 = f32[8,1,25920]{2,1,0:T(1,128)} reshape(f32[2880,2,36]{2,1,0:T(2,128)S(1)} %bitcast.80) | data formatting | bytes 1658880
  76.8 4.6 %all-to-all-start = ((f32[8,1,25920]{2,1,0:T(1,128)}), f32[8,1,25920]{2,1,0:T(1,128)S(1)}, u32[]{:S(2)}, u32[]{:S(2)}) async-start(f32[8,1,25920]{2,1,0:T(1,128)} %reshape.338), calls=%async_computation | async-start | bytes 1662976 | tf_op jit(solution)/shard_map/all_to_all | solution.py:102
  81.5 13.5 %all-to-all-done = f32[8,1,25920]{2,1,0:T(1,128)S(1)} async-done(((f32[8,1,25920]{2,1,0:T(1,128)}), f32[8,1,25920]{2,1,0:T(1,128)S(1)}, u32[]{:S(2)}, u32[]{:S(2)}) %all-to-all-start) | async-done | bytes 829472 | tf_op jit(solution)/shard_map/all_to_all | solution.py:102
  95.6 3.7 %reduce.8 = f32[8,25920]{1,0:T(8,128)} reduce(f32[8,1,25920]{2,1,0:T(1,128)S(1)} %all-to-all-done, f32[]{:T(128)} %broadcast.417), dimensions={1}, to_apply=%all_to_all.19.reduce_sub_computation | reduce | bytes 1658884 | tf_op jit(solution)/shard_map/all_to_all | solution.py:102
  99.4 6.2 %reshape.339 = f32[2880,2,36]{2,1,0:T(2,128)S(1)} reshape(f32[8,25920]{1,0:T(8,128)} %reduce.8) | data formatting | bytes 1658880
  111.7 3.5 %all-to-all-start.1 = ((f32[8,1024,16]{1,2,0:T(8,128)}), f32[8,1024,16]{1,2,0:T(8,128)S(1)}, u32[]{:S(2)}, u32[]{:S(2)}) async-start(f32[8,1024,16]{1,2,0:T(8,128)} %broadcast_in_dim.8), calls=%async_computation.1 | async-start | bytes 1048576 | tf_op jit(solution)/shard_map/all_to_all | solution.py:33
  115.3 10.2 %all-to-all-done.1 = f32[8,1024,16]{1,2,0:T(8,128)S(1)} async-done(((f32[8,1024,16]{1,2,0:T(8,128)}), f32[8,1024,16]{1,2,0:T(8,128)S(1)}, u32[]{:S(2)}, u32[]{:S(2)}) %all-to-all-start.1) | async-done | bytes 524320 | tf_op jit(solution)/shard_map/all_to_all | solution.py:33
  127.5 4.1 %collective-permute-start.9 = (f32[1,1024,16]{1,2,0:T(8,128)S(1)}, f32[1,1024,16]{1,2,0:T(8,128)S(1)}, u32[]{:S(2)}, u32[]{:S(2)}) collective-permute-start(f32[1,1024,16]{1,2,0:T(8,128)S(1)} %bitcast.84), channel_id=1, source_target_pairs={{8,0},{16,8},{24,16},{32,24},{40,32},{48,40},{56,48},{64,56},{72,6... | collective-permute-start | bytes 196616 | tf_op jit(solution)/shard_map/ppermute | solution.py:24
  142.0 8.5 %fusion.154 = (f32[36,360]{0,1:T(8,128)}, f32[16,360]{0,1:T(8,128)S(1)}, f32[16,36,360]{1,0,2:T(8,128)S(1)}) fusion(f32[16,36,360]{1,0,2:T(8,128)} %bitcast.79, f32[360,16,16]{1,2,0:T(8,128)} %copy.97, f32[36,360]{0,1:T(8,128)S(1)} %copy.96), kind=kOutput, calls=%fused_computation.212 | convolution fusion | flops 40623840 | bytes 2154240 | tf_op jit(solution)/shard_map/kdc,ckl->ldc/dot_general | solution.py:127
  152.3 3.5 %all-to-all-start.2 = ((f32[8,1024,16]{1,2,0:T(8,128)}), f32[8,1024,16]{1,2,0:T(8,128)S(1)}, u32[]{:S(2)}, u32[]{:S(2)}) async-start(f32[8,1024,16]{1,2,0:T(8,128)} %broadcast_in_dim.10), calls=%async_computation.2 | async-start | bytes 1048576 | tf_op jit(solution)/shard_map/all_to_all | solution.py:33
  157.4 8.6 %all-to-all-done.2 = f32[8,1024,16]{1,2,0:T(8,128)S(1)} async-done(((f32[8,1024,16]{1,2,0:T(8,128)}), f32[8,1024,16]{1,2,0:T(8,128)S(1)}, u32[]{:S(2)}, u32[]{:S(2)}) %all-to-all-start.2) | async-done | bytes 524320 | tf_op jit(solution)/shard_map/all_to_all | solution.py:33
  169.1 3.1 %collective-permute-start.11 = (f32[1,1024,16]{1,2,0:T(8,128)S(1)}, f32[1,1024,16]{1,2,0:T(8,128)S(1)}, u32[]{:S(2)}, u32[]{:S(2)}) collective-permute-start(f32[1,1024,16]{1,2,0:T(8,128)S(1)} %bitcast.86), channel_id=1, source_target_pairs={{8,0},{16,8},{24,16},{32,24},{40,32},{48,40},{56,48},{64,56},{72,6... | collective-permute-start | bytes 196616 | tf_op jit(solution)/shard_map/ppermute | solution.py:24
  173.2 5.4 %collective-permute-done.11 = f32[1,1024,16]{1,2,0:T(8,128)S(1)} collective-permute-done((f32[1,1024,16]{1,2,0:T(8,128)S(1)}, f32[1,1024,16]{1,2,0:T(8,128)S(1)}, u32[]{:S(2)}, u32[]{:S(2)}) %collective-permute-start.11) | collective-permute-done | bytes 65568 | tf_op jit(solution)/shard_map/ppermute | solution.py:24
  178.7 3.5 %fusion.30 = f32[360,16,16]{0,2,1:T(8,128)S(1)} fusion(s32[1024]{0:T(1024)S(1)} %bitcast.91, s32[1024]{0:T(1024)S(1)} %bitcast.92, s32[360]{0:T(512)} %copy-done.6, s32[360]{0:T(512)} %copy-done.7, f32[1024,16]{0,1:T(8,128)S(1)} %subtract_divide_fusion, f32[1024,16]{0,1:T(8,128)S(1)} %get-tuple-element.10), kind=kOutput, calls=%fused_computation.29 | convolution fusion | flops 1137778688 | bytes 510784 | tf_op jit(solution)/shard_map/dot_general | solution.py:123
  184.3 6.7 %bitcast_add_fusion = f32[16,36,360]{1,0,2:T(8,128)} fusion(f32[16,36,360]{1,0,2:T(8,128)S(1)} %get-tuple-element.81, f32[360,16,16]{1,2,0:T(8,128)} %copy.100, f32[36,360]{0,1:T(8,128)S(1)} %copy.99), kind=kOutput, calls=%fused_computation | convolution fusion | flops 40227840 | bytes 2079360 | tf_op jit(solution)/shard_map/kdc,ckl->ldc/dot_general | solution.py:127
  (93 shorter events, 57.7 us)
Async XLA Ops:
  1.4 10.2 %collective-permute-start = (f32[2,36,1,720]{3,1,2,0:T(8,128)S(1)}, f32[2,36,1,720]{3,1,2,0:T(8,128)S(1)}, u32[]{:S(2)}, u32[]{:S(2)}) collective-permute-start(f32[2,36,1,720]{3,1,2,0:T(8,128)S(1)} %get-tuple-element.51), channel_id=1, source_target_pairs={{0,8},{8,16},{16,24},{24,32},{32,40},{40,48},{48,56},{56,64},{64,7... | collective-permute-start | bytes 622088 | tf_op jit(solution)/shard_map/ppermute | solution.py:22
  6.3 12.6 %collective-permute-start.1 = (f32[2,36,1,720]{3,1,2,0:T(8,128)S(1)}, f32[2,36,1,720]{3,1,2,0:T(8,128)S(1)}, u32[]{:S(2)}, u32[]{:S(2)}) collective-permute-start(f32[2,36,1,720]{3,1,2,0:T(8,128)S(1)} %get-tuple-element.52), channel_id=1, source_target_pairs={{8,0},{16,8},{24,16},{32,24},{40,32},{48,40},{56,48},{64,56},{72,6... | collective-permute-start | bytes 622088 | tf_op jit(solution)/shard_map/ppermute | solution.py:24
  8.5 0.7 copy-start.1
  8.5 0.7 copy-start.2
  20.5 8.4 %collective-permute-start.2 = (f32[2,36,1,720]{3,1,2,0:T(8,128)S(1)}, f32[2,36,1,720]{3,1,2,0:T(8,128)S(1)}, u32[]{:S(2)}, u32[]{:S(2)}) collective-permute-start(f32[2,36,1,720]{3,1,2,0:T(8,128)S(1)} %get-tuple-element.41), channel_id=1, source_target_pairs={{0,8},{8,16},{16,24},{24,32},{32,40},{40,48},{48,56},{56,64},{64,7... | collective-permute-start | bytes 622088 | tf_op jit(solution)/shard_map/ppermute | solution.py:22
  22.5 11.7 %collective-permute-start.3 = (f32[2,36,1,720]{3,1,2,0:T(8,128)S(1)}, f32[2,36,1,720]{3,1,2,0:T(8,128)S(1)}, u32[]{:S(2)}, u32[]{:S(2)}) collective-permute-start(f32[2,36,1,720]{3,1,2,0:T(8,128)S(1)} %get-tuple-element.42), channel_id=1, source_target_pairs={{8,0},{16,8},{24,16},{32,24},{40,32},{48,40},{56,48},{64,56},{72,6... | collective-permute-start | bytes 622088 | tf_op jit(solution)/shard_map/ppermute | solution.py:24
  35.7 8.1 %collective-permute-start.4 = (f32[2,36,1,720]{3,1,2,0:T(8,128)S(1)}, f32[2,36,1,720]{3,1,2,0:T(8,128)S(1)}, u32[]{:S(2)}, u32[]{:S(2)}) collective-permute-start(f32[2,36,1,720]{3,1,2,0:T(8,128)S(1)} %get-tuple-element.31), channel_id=1, source_target_pairs={{0,8},{8,16},{16,24},{24,32},{32,40},{40,48},{48,56},{56,64},{64,7... | collective-permute-start | bytes 622088 | tf_op jit(solution)/shard_map/ppermute | solution.py:22
  37.7 11.4 %collective-permute-start.5 = (f32[2,36,1,720]{3,1,2,0:T(8,128)S(1)}, f32[2,36,1,720]{3,1,2,0:T(8,128)S(1)}, u32[]{:S(2)}, u32[]{:S(2)}) collective-permute-start(f32[2,36,1,720]{3,1,2,0:T(8,128)S(1)} %get-tuple-element.32), channel_id=1, source_target_pairs={{8,0},{16,8},{24,16},{32,24},{40,32},{48,40},{56,48},{64,56},{72,6... | collective-permute-start | bytes 622088 | tf_op jit(solution)/shard_map/ppermute | solution.py:24
  50.6 8.1 %collective-permute-start.6 = (f32[2,36,1,720]{3,1,2,0:T(8,128)S(1)}, f32[2,36,1,720]{3,1,2,0:T(8,128)S(1)}, u32[]{:S(2)}, u32[]{:S(2)}) collective-permute-start(f32[2,36,1,720]{3,1,2,0:T(8,128)S(1)} %get-tuple-element.21), channel_id=1, source_target_pairs={{0,8},{8,16},{16,24},{24,32},{32,40},{40,48},{48,56},{56,64},{64,7... | collective-permute-start | bytes 622088 | tf_op jit(solution)/shard_map/ppermute | solution.py:22
  52.6 11.4 %collective-permute-start.7 = (f32[2,36,1,720]{3,1,2,0:T(8,128)S(1)}, f32[2,36,1,720]{3,1,2,0:T(8,128)S(1)}, u32[]{:S(2)}, u32[]{:S(2)}) collective-permute-start(f32[2,36,1,720]{3,1,2,0:T(8,128)S(1)} %get-tuple-element.22), channel_id=1, source_target_pairs={{8,0},{16,8},{24,16},{32,24},{40,32},{48,40},{56,48},{64,56},{72,6... | collective-permute-start | bytes 622088 | tf_op jit(solution)/shard_map/ppermute | solution.py:24
  76.8 4.6 %copy-start.5 = (s32[2,1024]{1,0:T(2,128)S(1)}, s32[2,1024]{1,0:T(2,128)}, u32[]{:S(2)}) copy-start(s32[2,1024]{1,0:T(2,128)} %param.9) | copy-start | bytes 24580
  76.8 18.2 %all-to-all-start = ((f32[8,1,25920]{2,1,0:T(1,128)}), f32[8,1,25920]{2,1,0:T(1,128)S(1)}, u32[]{:S(2)}, u32[]{:S(2)}) async-start(f32[8,1,25920]{2,1,0:T(1,128)} %reshape.338), calls=%async_computation | async-start | bytes 1662976 | tf_op jit(solution)/shard_map/all_to_all | solution.py:102
  108.6 6.7 %copy-start.3 = (f32[2,1024]{1,0:T(2,128)S(1)}, f32[2,1024]{1,0:T(2,128)}, u32[]{:S(2)}) copy-start(f32[2,1024]{1,0:T(2,128)} %param.10) | copy-start | bytes 24580
  108.6 6.7 %copy-start.4 = (f32[2,1024]{1,0:T(2,128)S(1)}, f32[2,1024]{1,0:T(2,128)}, u32[]{:S(2)}) copy-start(f32[2,1024]{1,0:T(2,128)} %param.11) | copy-start | bytes 24580
  110.0 21.7 %copy-start = (f32[2,36,8,360]{3,2,0,1:T(8,128)S(1)}, f32[2,36,8,360]{3,2,0,1:T(8,128)}, u32[]{:S(2)}) copy-start(f32[2,36,8,360]{3,2,0,1:T(8,128)} %copy.103) | copy-start | bytes 2488324
  111.7 13.8 %all-to-all-start.1 = ((f32[8,1024,16]{1,2,0:T(8,128)}), f32[8,1024,16]{1,2,0:T(8,128)S(1)}, u32[]{:S(2)}, u32[]{:S(2)}) async-start(f32[8,1024,16]{1,2,0:T(8,128)} %broadcast_in_dim.8), calls=%async_computation.1 | async-start | bytes 1048576 | tf_op jit(solution)/shard_map/all_to_all | solution.py:33
  115.3 21.8 %copy-start.6 = (s32[360]{0:T(512)}, s32[360]{0:T(512)S(1)}, u32[]{:S(2)}) copy-start(s32[360]{0:T(512)S(1)} %get-tuple-element.84) | copy-start | bytes 4324
  115.3 21.8 %copy-start.7 = (s32[360]{0:T(512)}, s32[360]{0:T(512)S(1)}, u32[]{:S(2)}) copy-start(s32[360]{0:T(512)S(1)} %get-tuple-element.85) | copy-start | bytes 4324
  125.5 9.1 %collective-permute-start.8 = (f32[1,1024,16]{1,2,0:T(8,128)S(1)}, f32[1,1024,16]{1,2,0:T(8,128)S(1)}, u32[]{:S(2)}, u32[]{:S(2)}) collective-permute-start(f32[1,1024,16]{1,2,0:T(8,128)S(1)} %bitcast.83), channel_id=1, source_target_pairs={{0,8},{8,16},{16,24},{24,32},{32,40},{40,48},{48,56},{56,64},{64,7... | collective-permute-start | bytes 196616 | tf_op jit(solution)/shard_map/ppermute | solution.py:22
  127.5 9.5 %collective-permute-start.9 = (f32[1,1024,16]{1,2,0:T(8,128)S(1)}, f32[1,1024,16]{1,2,0:T(8,128)S(1)}, u32[]{:S(2)}, u32[]{:S(2)}) collective-permute-start(f32[1,1024,16]{1,2,0:T(8,128)S(1)} %bitcast.84), channel_id=1, source_target_pairs={{8,0},{16,8},{24,16},{32,24},{40,32},{48,40},{56,48},{64,56},{72,6... | collective-permute-start | bytes 196616 | tf_op jit(solution)/shard_map/ppermute | solution.py:24
  152.3 13.8 %all-to-all-start.2 = ((f32[8,1024,16]{1,2,0:T(8,128)}), f32[8,1024,16]{1,2,0:T(8,128)S(1)}, u32[]{:S(2)}, u32[]{:S(2)}) async-start(f32[8,1024,16]{1,2,0:T(8,128)} %broadcast_in_dim.10), calls=%async_computation.2 | async-start | bytes 1048576 | tf_op jit(solution)/shard_map/all_to_all | solution.py:33
  166.1 7.1 %collective-permute-start.10 = (f32[1,1024,16]{1,2,0:T(8,128)S(1)}, f32[1,1024,16]{1,2,0:T(8,128)S(1)}, u32[]{:S(2)}, u32[]{:S(2)}) collective-permute-start(f32[1,1024,16]{1,2,0:T(8,128)S(1)} %bitcast.85), channel_id=1, source_target_pairs={{0,8},{8,16},{16,24},{24,32},{32,40},{40,48},{48,56},{56,64},{64,7... | collective-permute-start | bytes 196616 | tf_op jit(solution)/shard_map/ppermute | solution.py:22
  169.1 9.5 %collective-permute-start.11 = (f32[1,1024,16]{1,2,0:T(8,128)S(1)}, f32[1,1024,16]{1,2,0:T(8,128)S(1)}, u32[]{:S(2)}, u32[]{:S(2)}) collective-permute-start(f32[1,1024,16]{1,2,0:T(8,128)S(1)} %bitcast.86), channel_id=1, source_target_pairs={{8,0},{16,8},{24,16},{32,24},{40,32},{48,40},{56,48},{64,56},{72,6... | collective-permute-start | bytes 196616 | tf_op jit(solution)/shard_map/ppermute | solution.py:24
where the time goes:
time: 195 us; the launch traced here: 194 us
  waiting for transfers between devices  72 us (37%)
  starting transfers between devices  48.2 us (25%)
  local copies, waits for them, and re-layouts  38.8 us (20%)
  matrix products  23.2 us (12%)
  other arithmetic  11.4 us (6%)
    ppermute x6, waiting for transfers between devices, padded_2(): lax.ppermute(head, axis, [((i + 1) % count, i) for i in range(ends)])  30.8 us
    ppermute x6, starting transfers between devices, padded_2(): lax.ppermute(head, axis, [((i + 1) % count, i) for i in range(ends)])  21 us
    all_to_all x2, waiting for transfers between devices, copy_for_each(): lax.all_to_all(jnp.broadcast_to(array[None], (devices, *array.shape)), ax...  18.8 us
    ppermute x6, starting transfers between devices, padded_2(): lax.ppermute(tail, axis, [(i, (i + 1) % count) for i in range(ends)])  15.6 us
    dot_general x2, matrix products, per_device(): state = state + jnp.einsum('kdc,ckl->ldc', deviation, gain, precision=HIGH)  15.1 us
    unnamed x19, local copies, waits for them, and re-layouts  14.1 us
    all_to_all x1, waiting for transfers between devices, per_device(): lax.all_to_all(energy.reshape(local_members, directions, rows * width), '...  13.5 us
    ppermute x6, waiting for transfers between devices, padded_2(): lax.ppermute(tail, axis, [(i, (i + 1) % count) for i in range(ends)])  8.82 us
  transfers between devices with their start and end apart: 15, of which 13 were waited for; matrix products, arithmetic and copies ran while one was open for 4% of the time, Pallas kernels for 0%

commit v1 on v0

--- a/solution.py
+++ b/solution.py
@@ -9,6 +9,14 @@
 BATCHES = 2
 LOC = 4
 HIGH = lax.Precision.HIGHEST
+
+
+def supply_all_quotas(array_in, ax_name):
+    w1 = jax.lax.axis_size(ax_name)
+    current_block = jnp.split(array_in, w1, 2)
+    local_out = jnp.stack(current_block)
+    t_next = jax.lax.all_to_all(local_out, axis_name=ax_name, split_axis=0, concat_axis=0)
+    return jnp.concatenate(t_next, 0)
 
 
 def padded_2(cells, sides, width):
@@ -99,13 +107,7 @@
     for step in range(STEPS):
         padded = padded_2(energy, (("space", 2),), 1)
         energy = transport(padded, group_speed, turning_rate, cosines, sines)
-    state = lax.all_to_all(
-        energy.reshape(local_members, directions, rows * width),
-        "member",
-        split_axis=2,
-        concat_axis=0,
-        tiled=True,
-    )
+    state = supply_all_quotas(energy.reshape(local_members, directions, rows * width), "member")
     members, directions, owned = state.shape
     first_cell = (
         lax.axis_index("space") * lax.axis_size("member") + lax.axis_index("member")

time: 195 us -> 178 us (0.913)
  the two profiles are of different devices: /device:TPU:230 before, /device:TPU:102 now
where the time goes in v1:
time: 178 us; the launch traced here: 177 us
  waiting for transfers between devices  72.5 us (41%)
  starting transfers between devices  47.9 us (27%)
  local copies, waits for them, and re-layouts  26.8 us (15%)
  matrix products  23.2 us (13%)
  other arithmetic  5.75 us (3%)
    ppermute x6, waiting for transfers between devices, padded_2(): lax.ppermute(head, axis, [((i + 1) % count, i) for i in range(ends)])  30.9 us
    ppermute x6, starting transfers between devices, padded_2(): lax.ppermute(head, axis, [((i + 1) % count, i) for i in range(ends)])  20.3 us
    all_to_all x2, waiting for transfers between devices, copy_for_each(): lax.all_to_all(jnp.broadcast_to(array[None], (devices, *array.shape)), ax...  18.8 us
    ppermute x6, starting transfers between devices, padded_2(): lax.ppermute(tail, axis, [(i, (i + 1) % count) for i in range(ends)])  16.2 us
    dot_general x2, matrix products, per_device(): state = state + jnp.einsum('kdc,ckl->ldc', deviation, gain, precision=HIGH)  15.1 us
    all_to_all x1, waiting for transfers between devices, supply_all_quotas(): jax.lax.all_to_all(local_out, axis_name=ax_name, split_axis=0, concat_axi...  14.1 us
    ppermute x6, waiting for transfers between devices, padded_2(): lax.ppermute(tail, axis, [(i, (i + 1) % count) for i in range(ends)])  8.82 us
    unnamed x22, local copies, waits for them, and re-layouts  7.27 us
  transfers between devices with their start and end apart: 15, of which 13 were waited for; matrix products, arithmetic and copies ran while one was open for 4% of the time, Pallas kernels for 0%

profile of v1, /device:TPU:102, one launch (start us, length us, event | category | flops | bytes accessed | tf_op | source)
XLA Modules:
  0.0 176.7 jit_solution(9308034760938547195)
XLA Ops:
  1.4 5.0 %collective-permute-start = (f32[2,36,1,720]{3,1,2,0:T(8,128)S(1)}, f32[2,36,1,720]{3,1,2,0:T(8,128)S(1)}, u32[]{:S(2)}, u32[]{:S(2)}) collective-permute-start(f32[2,36,1,720]{3,1,2,0:T(8,128)S(1)} %get-tuple-element.51), channel_id=1, source_target_pairs={{0,8},{8,16},{16,24},{24,32},{32,40},{40,48},{48,56},{56,64},{64,7... | collective-permute-start | bytes 622088 | tf_op jit(solution)/shard_map/ppermute | solution.py:30
  11.5 7.4 %collective-permute-done.1 = f32[2,36,1,720]{3,1,2,0:T(8,128)S(1)} collective-permute-done((f32[2,36,1,720]{3,1,2,0:T(8,128)S(1)}, f32[2,36,1,720]{3,1,2,0:T(8,128)S(1)}, u32[]{:S(2)}, u32[]{:S(2)}) %collective-permute-start.1) | collective-permute-done | bytes 207392 | tf_op jit(solution)/shard_map/ppermute | solution.py:32
  22.5 3.9 %collective-permute-start.3 = (f32[2,36,1,720]{3,1,2,0:T(8,128)S(1)}, f32[2,36,1,720]{3,1,2,0:T(8,128)S(1)}, u32[]{:S(2)}, u32[]{:S(2)}) collective-permute-start(f32[2,36,1,720]{3,1,2,0:T(8,128)S(1)} %get-tuple-element.42), channel_id=1, source_target_pairs={{8,0},{16,8},{24,16},{32,24},{40,32},{48,40},{56,48},{64,56},{72,6... | collective-permute-start | bytes 622088 | tf_op jit(solution)/shard_map/ppermute | solution.py:32
  26.4 2.5 %collective-permute-done.2 = f32[2,36,1,720]{3,1,2,0:T(8,128)S(1)} collective-permute-done((f32[2,36,1,720]{3,1,2,0:T(8,128)S(1)}, f32[2,36,1,720]{3,1,2,0:T(8,128)S(1)}, u32[]{:S(2)}, u32[]{:S(2)}) %collective-permute-start.2) | collective-permute-done | bytes 207392 | tf_op jit(solution)/shard_map/ppermute | solution.py:30
  28.9 5.2 %collective-permute-done.3 = f32[2,36,1,720]{3,1,2,0:T(8,128)S(1)} collective-permute-done((f32[2,36,1,720]{3,1,2,0:T(8,128)S(1)}, f32[2,36,1,720]{3,1,2,0:T(8,128)S(1)}, u32[]{:S(2)}, u32[]{:S(2)}) %collective-permute-start.3) | collective-permute-done | bytes 207392 | tf_op jit(solution)/shard_map/ppermute | solution.py:32
  37.7 3.9 %collective-permute-start.5 = (f32[2,36,1,720]{3,1,2,0:T(8,128)S(1)}, f32[2,36,1,720]{3,1,2,0:T(8,128)S(1)}, u32[]{:S(2)}, u32[]{:S(2)}) collective-permute-start(f32[2,36,1,720]{3,1,2,0:T(8,128)S(1)} %get-tuple-element.32), channel_id=1, source_target_pairs={{8,0},{16,8},{24,16},{32,24},{40,32},{48,40},{56,48},{64,56},{72,6... | collective-permute-start | bytes 622088 | tf_op jit(solution)/shard_map/ppermute | solution.py:32
  43.8 5.2 %collective-permute-done.5 = f32[2,36,1,720]{3,1,2,0:T(8,128)S(1)} collective-permute-done((f32[2,36,1,720]{3,1,2,0:T(8,128)S(1)}, f32[2,36,1,720]{3,1,2,0:T(8,128)S(1)}, u32[]{:S(2)}, u32[]{:S(2)}) %collective-permute-start.5) | collective-permute-done | bytes 207392 | tf_op jit(solution)/shard_map/ppermute | solution.py:32
  52.6 3.9 %collective-permute-start.7 = (f32[2,36,1,720]{3,1,2,0:T(8,128)S(1)}, f32[2,36,1,720]{3,1,2,0:T(8,128)S(1)}, u32[]{:S(2)}, u32[]{:S(2)}) collective-permute-start(f32[2,36,1,720]{3,1,2,0:T(8,128)S(1)} %get-tuple-element.22), channel_id=1, source_target_pairs={{8,0},{16,8},{24,16},{32,24},{40,32},{48,40},{56,48},{64,56},{72,6... | collective-permute-start | bytes 622088 | tf_op jit(solution)/shard_map/ppermute | solution.py:32
  58.7 5.2 %collective-permute-done.7 = f32[2,36,1,720]{3,1,2,0:T(8,128)S(1)} collective-permute-done((f32[2,36,1,720]{3,1,2,0:T(8,128)S(1)}, f32[2,36,1,720]{3,1,2,0:T(8,128)S(1)}, u32[]{:S(2)}, u32[]{:S(2)}) %collective-permute-start.7) | collective-permute-done | bytes 207392 | tf_op jit(solution)/shard_map/ppermute | solution.py:32
  72.9 4.5 %all-to-all-start = ((f32[8,2,36,360]{3,1,2,0:T(2,128)}), f32[8,2,36,360]{3,1,2,0:T(2,128)S(1)}, u32[]{:S(2)}, u32[]{:S(2)}) async-start(f32[8,2,36,360]{3,1,2,0:T(2,128)} %fusion.131), calls=%async_computation | async-start | bytes 1769472 | tf_op jit(solution)/shard_map/all_to_all | solution.py:18
  77.4 14.1 %all-to-all-done = f32[8,2,36,360]{3,1,2,0:T(2,128)S(1)} async-done(((f32[8,2,36,360]{3,1,2,0:T(2,128)}), f32[8,2,36,360]{3,1,2,0:T(2,128)S(1)}, u32[]{:S(2)}, u32[]{:S(2)}) %all-to-all-start) | async-done | bytes 829472 | tf_op jit(solution)/shard_map/all_to_all | solution.py:18
  93.8 3.5 %all-to-all-start.1 = ((f32[8,1024,16]{1,2,0:T(8,128)}), f32[8,1024,16]{1,2,0:T(8,128)S(1)}, u32[]{:S(2)}, u32[]{:S(2)}) async-start(f32[8,1024,16]{1,2,0:T(8,128)} %broadcast_in_dim.8), calls=%async_computation.1 | async-start | bytes 1048576 | tf_op jit(solution)/shard_map/all_to_all | solution.py:41
  97.4 10.2 %all-to-all-done.1 = f32[8,1024,16]{1,2,0:T(8,128)S(1)} async-done(((f32[8,1024,16]{1,2,0:T(8,128)}), f32[8,1024,16]{1,2,0:T(8,128)S(1)}, u32[]{:S(2)}, u32[]{:S(2)}) %all-to-all-start.1) | async-done | bytes 524320 | tf_op jit(solution)/shard_map/all_to_all | solution.py:41
  109.5 4.1 %collective-permute-start.9 = (f32[1,1024,16]{1,2,0:T(8,128)S(1)}, f32[1,1024,16]{1,2,0:T(8,128)S(1)}, u32[]{:S(2)}, u32[]{:S(2)}) collective-permute-start(f32[1,1024,16]{1,2,0:T(8,128)S(1)} %bitcast.108), channel_id=1, source_target_pairs={{8,0},{16,8},{24,16},{32,24},{40,32},{48,40},{56,48},{64,56},{72,6... | collective-permute-start | bytes 196616 | tf_op jit(solution)/shard_map/ppermute | solution.py:32
  113.7 3.6 %copy.69 = f32[8,2,36,360]{2,1,0,3:T(2,128)} copy(f32[8,2,36,360]{3,1,2,0:T(2,128)S(1)} %all-to-all-done) | data formatting | bytes 1658880 | tf_op jit(solution)/shard_map/all_to_all | solution.py:18
  119.1 2.8 %fusion.20 = f32[360,16,16]{0,2,1:T(8,128)S(1)} fusion(s32[1024]{0:T(1024)S(1)} %bitcast.118, s32[360]{0:T(512)S(1)} %get-tuple-element.84, s32[1024]{0:T(1024)S(1)} %bitcast.119, s32[360]{0:T(512)S(1)} %get-tuple-element.85, f32[1024,16]{0,1:T(8,128)S(1)} %subtract_divide_fusion.1, f32[1024,16]{0,1:T(8,128)S(1)} %get-tuple-element.12), kind=kOutput, calls=%fused_computation.20 | convolution fusion | flops 1137778688 | bytes 510784 | tf_op jit(solution)/shard_map/dot_general | solution.py:125
  124.1 8.5 %fusion.162 = (f32[36,360]{0,1:T(8,128)}, f32[16,360]{0,1:T(8,128)S(1)}, f32[16,36,360]{1,0,2:T(8,128)S(1)}) fusion(f32[16,36,360]{1,0,2:T(8,128)} %bitcast.106, f32[360,16,16]{1,2,0:T(8,128)} %copy.71, f32[36,360]{0,1:T(8,128)S(1)} %copy.70), kind=kOutput, calls=%fused_computation.226 | convolution fusion | flops 40623840 | bytes 2154240 | tf_op jit(solution)/shard_map/kdc,ckl->ldc/dot_general | solution.py:129
  134.3 3.5 %all-to-all-start.2 = ((f32[8,1024,16]{1,2,0:T(8,128)}), f32[8,1024,16]{1,2,0:T(8,128)S(1)}, u32[]{:S(2)}, u32[]{:S(2)}) async-start(f32[8,1024,16]{1,2,0:T(8,128)} %broadcast_in_dim.10), calls=%async_computation.2 | async-start | bytes 1048576 | tf_op jit(solution)/shard_map/all_to_all | solution.py:41
  139.5 8.6 %all-to-all-done.2 = f32[8,1024,16]{1,2,0:T(8,128)S(1)} async-done(((f32[8,1024,16]{1,2,0:T(8,128)}), f32[8,1024,16]{1,2,0:T(8,128)S(1)}, u32[]{:S(2)}, u32[]{:S(2)}) %all-to-all-start.2) | async-done | bytes 524320 | tf_op jit(solution)/shard_map/all_to_all | solution.py:41
  148.1 3.6 %collective-permute-start.10 = (f32[1,1024,16]{1,2,0:T(8,128)S(1)}, f32[1,1024,16]{1,2,0:T(8,128)S(1)}, u32[]{:S(2)}, u32[]{:S(2)}) collective-permute-start(f32[1,1024,16]{1,2,0:T(8,128)S(1)} %bitcast.109), channel_id=1, source_target_pairs={{0,8},{8,16},{16,24},{24,32},{32,40},{40,48},{48,56},{56,64},{64,7... | collective-permute-start | bytes 196616 | tf_op jit(solution)/shard_map/ppermute | solution.py:30
  155.2 6.0 %collective-permute-done.11 = f32[1,1024,16]{1,2,0:T(8,128)S(1)} collective-permute-done((f32[1,1024,16]{1,2,0:T(8,128)S(1)}, f32[1,1024,16]{1,2,0:T(8,128)S(1)}, u32[]{:S(2)}, u32[]{:S(2)}) %collective-permute-start.11) | collective-permute-done | bytes 65568 | tf_op jit(solution)/shard_map/ppermute | solution.py:32
  161.3 3.5 %fusion.30 = f32[360,16,16]{0,2,1:T(8,128)S(1)} fusion(s32[1024]{0:T(1024)S(1)} %bitcast.115, s32[1024]{0:T(1024)S(1)} %bitcast.116, s32[360]{0:T(512)} %copy-done.5, s32[360]{0:T(512)} %copy-done.6, f32[1024,16]{0,1:T(8,128)S(1)} %subtract_divide_fusion, f32[1024,16]{0,1:T(8,128)S(1)} %get-tuple-element.10), kind=kOutput, calls=%fused_computation.29 | convolution fusion | flops 1137778688 | bytes 510784 | tf_op jit(solution)/shard_map/dot_general | solution.py:125
  166.9 6.7 %bitcast_add_fusion = f32[16,36,360]{1,0,2:T(8,128)} fusion(f32[16,36,360]{1,0,2:T(8,128)S(1)} %get-tuple-element.81, f32[360,16,16]{1,2,0:T(8,128)} %copy.74, f32[36,360]{0,1:T(8,128)S(1)} %copy.73), kind=kOutput, calls=%fused_computation | convolution fusion | flops 40227840 | bytes 2079360 | tf_op jit(solution)/shard_map/kdc,ckl->ldc/dot_general | solution.py:129
  173.6 3.1 %copy.75 = f32[16,36,360]{2,0,1:T(8,128)} copy(f32[16,36,360]{1,0,2:T(8,128)} %bitcast_add_fusion) | data formatting | bytes 1658880 | tf_op jit(solution)/shard_map/add | solution.py:129
  (94 shorter events, 47.6 us)
Async XLA Ops:
  1.4 10.2 %collective-permute-start = (f32[2,36,1,720]{3,1,2,0:T(8,128)S(1)}, f32[2,36,1,720]{3,1,2,0:T(8,128)S(1)}, u32[]{:S(2)}, u32[]{:S(2)}) collective-permute-start(f32[2,36,1,720]{3,1,2,0:T(8,128)S(1)} %get-tuple-element.51), channel_id=1, source_target_pairs={{0,8},{8,16},{16,24},{24,32},{32,40},{40,48},{48,56},{56,64},{64,7... | collective-permute-start | bytes 622088 | tf_op jit(solution)/shard_map/ppermute | solution.py:30
  6.3 12.6 %collective-permute-start.1 = (f32[2,36,1,720]{3,1,2,0:T(8,128)S(1)}, f32[2,36,1,720]{3,1,2,0:T(8,128)S(1)}, u32[]{:S(2)}, u32[]{:S(2)}) collective-permute-start(f32[2,36,1,720]{3,1,2,0:T(8,128)S(1)} %get-tuple-element.52), channel_id=1, source_target_pairs={{8,0},{16,8},{24,16},{32,24},{40,32},{48,40},{56,48},{64,56},{72,6... | collective-permute-start | bytes 622088 | tf_op jit(solution)/shard_map/ppermute | solution.py:32
  8.5 0.7 copy-start
  8.5 0.7 copy-start.1
  20.5 8.4 %collective-permute-start.2 = (f32[2,36,1,720]{3,1,2,0:T(8,128)S(1)}, f32[2,36,1,720]{3,1,2,0:T(8,128)S(1)}, u32[]{:S(2)}, u32[]{:S(2)}) collective-permute-start(f32[2,36,1,720]{3,1,2,0:T(8,128)S(1)} %get-tuple-element.41), channel_id=1, source_target_pairs={{0,8},{8,16},{16,24},{24,32},{32,40},{40,48},{48,56},{56,64},{64,7... | collective-permute-start | bytes 622088 | tf_op jit(solution)/shard_map/ppermute | solution.py:30
  22.5 11.7 %collective-permute-start.3 = (f32[2,36,1,720]{3,1,2,0:T(8,128)S(1)}, f32[2,36,1,720]{3,1,2,0:T(8,128)S(1)}, u32[]{:S(2)}, u32[]{:S(2)}) collective-permute-start(f32[2,36,1,720]{3,1,2,0:T(8,128)S(1)} %get-tuple-element.42), channel_id=1, source_target_pairs={{8,0},{16,8},{24,16},{32,24},{40,32},{48,40},{56,48},{64,56},{72,6... | collective-permute-start | bytes 622088 | tf_op jit(solution)/shard_map/ppermute | solution.py:32
  35.7 8.1 %collective-permute-start.4 = (f32[2,36,1,720]{3,1,2,0:T(8,128)S(1)}, f32[2,36,1,720]{3,1,2,0:T(8,128)S(1)}, u32[]{:S(2)}, u32[]{:S(2)}) collective-permute-start(f32[2,36,1,720]{3,1,2,0:T(8,128)S(1)} %get-tuple-element.31), channel_id=1, source_target_pairs={{0,8},{8,16},{16,24},{24,32},{32,40},{40,48},{48,56},{56,64},{64,7... | collective-permute-start | bytes 622088 | tf_op jit(solution)/shard_map/ppermute | solution.py:30
  37.7 11.4 %collective-permute-start.5 = (f32[2,36,1,720]{3,1,2,0:T(8,128)S(1)}, f32[2,36,1,720]{3,1,2,0:T(8,128)S(1)}, u32[]{:S(2)}, u32[]{:S(2)}) collective-permute-start(f32[2,36,1,720]{3,1,2,0:T(8,128)S(1)} %get-tuple-element.32), channel_id=1, source_target_pairs={{8,0},{16,8},{24,16},{32,24},{40,32},{48,40},{56,48},{64,56},{72,6... | collective-permute-start | bytes 622088 | tf_op jit(solution)/shard_map/ppermute | solution.py:32
  50.6 8.1 %collective-permute-start.6 = (f32[2,36,1,720]{3,1,2,0:T(8,128)S(1)}, f32[2,36,1,720]{3,1,2,0:T(8,128)S(1)}, u32[]{:S(2)}, u32[]{:S(2)}) collective-permute-start(f32[2,36,1,720]{3,1,2,0:T(8,128)S(1)} %get-tuple-element.21), channel_id=1, source_target_pairs={{0,8},{8,16},{16,24},{24,32},{32,40},{40,48},{48,56},{56,64},{64,7... | collective-permute-start | bytes 622088 | tf_op jit(solution)/shard_map/ppermute | solution.py:30
  52.6 11.4 %collective-permute-start.7 = (f32[2,36,1,720]{3,1,2,0:T(8,128)S(1)}, f32[2,36,1,720]{3,1,2,0:T(8,128)S(1)}, u32[]{:S(2)}, u32[]{:S(2)}) collective-permute-start(f32[2,36,1,720]{3,1,2,0:T(8,128)S(1)} %get-tuple-element.22), channel_id=1, source_target_pairs={{8,0},{16,8},{24,16},{32,24},{40,32},{48,40},{56,48},{64,56},{72,6... | collective-permute-start | bytes 622088 | tf_op jit(solution)/shard_map/ppermute | solution.py:32
  68.7 8.6 %copy-start.4 = (s32[2,1024]{1,0:T(2,128)S(1)}, s32[2,1024]{1,0:T(2,128)}, u32[]{:S(2)}) copy-start(s32[2,1024]{1,0:T(2,128)} %param.9) | copy-start | bytes 24580
  72.9 18.7 %all-to-all-start = ((f32[8,2,36,360]{3,1,2,0:T(2,128)}), f32[8,2,36,360]{3,1,2,0:T(2,128)S(1)}, u32[]{:S(2)}, u32[]{:S(2)}) async-start(f32[8,2,36,360]{3,1,2,0:T(2,128)} %fusion.131), calls=%async_computation | async-start | bytes 1769472 | tf_op jit(solution)/shard_map/all_to_all | solution.py:18
  77.4 19.9 %copy-start.2 = (f32[2,1024]{1,0:T(2,128)S(1)}, f32[2,1024]{1,0:T(2,128)}, u32[]{:S(2)}) copy-start(f32[2,1024]{1,0:T(2,128)} %param.10) | copy-start | bytes 24580
  77.4 19.9 %copy-start.3 = (f32[2,1024]{1,0:T(2,128)S(1)}, f32[2,1024]{1,0:T(2,128)}, u32[]{:S(2)}) copy-start(f32[2,1024]{1,0:T(2,128)} %param.11) | copy-start | bytes 24580
  93.8 13.8 %all-to-all-start.1 = ((f32[8,1024,16]{1,2,0:T(8,128)}), f32[8,1024,16]{1,2,0:T(8,128)S(1)}, u32[]{:S(2)}, u32[]{:S(2)}) async-start(f32[8,1024,16]{1,2,0:T(8,128)} %broadcast_in_dim.8), calls=%async_computation.1 | async-start | bytes 1048576 | tf_op jit(solution)/shard_map/all_to_all | solution.py:41
  97.3 21.8 %copy-start.5 = (s32[360]{0:T(512)}, s32[360]{0:T(512)S(1)}, u32[]{:S(2)}) copy-start(s32[360]{0:T(512)S(1)} %get-tuple-element.84) | copy-start | bytes 4324
  97.3 21.8 %copy-start.6 = (s32[360]{0:T(512)}, s32[360]{0:T(512)S(1)}, u32[]{:S(2)}) copy-start(s32[360]{0:T(512)S(1)} %get-tuple-element.85) | copy-start | bytes 4324
  107.6 9.8 %collective-permute-start.8 = (f32[1,1024,16]{1,2,0:T(8,128)S(1)}, f32[1,1024,16]{1,2,0:T(8,128)S(1)}, u32[]{:S(2)}, u32[]{:S(2)}) collective-permute-start(f32[1,1024,16]{1,2,0:T(8,128)S(1)} %bitcast.107), channel_id=1, source_target_pairs={{0,8},{8,16},{16,24},{24,32},{32,40},{40,48},{48,56},{56,64},{64,7... | collective-permute-start | bytes 196616 | tf_op jit(solution)/shard_map/ppermute | solution.py:30
  109.5 9.5 %collective-permute-start.9 = (f32[1,1024,16]{1,2,0:T(8,128)S(1)}, f32[1,1024,16]{1,2,0:T(8,128)S(1)}, u32[]{:S(2)}, u32[]{:S(2)}) collective-permute-start(f32[1,1024,16]{1,2,0:T(8,128)S(1)} %bitcast.108), channel_id=1, source_target_pairs={{8,0},{16,8},{24,16},{32,24},{40,32},{48,40},{56,48},{64,56},{72,6... | collective-permute-start | bytes 196616 | tf_op jit(solution)/shard_map/ppermute | solution.py:32
  134.3 13.8 %all-to-all-start.2 = ((f32[8,1024,16]{1,2,0:T(8,128)}), f32[8,1024,16]{1,2,0:T(8,128)S(1)}, u32[]{:S(2)}, u32[]{:S(2)}) async-start(f32[8,1024,16]{1,2,0:T(8,128)} %broadcast_in_dim.10), calls=%async_computation.2 | async-start | bytes 1048576 | tf_op jit(solution)/shard_map/all_to_all | solution.py:41
  148.1 7.0 %collective-permute-start.10 = (f32[1,1024,16]{1,2,0:T(8,128)S(1)}, f32[1,1024,16]{1,2,0:T(8,128)S(1)}, u32[]{:S(2)}, u32[]{:S(2)}) collective-permute-start(f32[1,1024,16]{1,2,0:T(8,128)S(1)} %bitcast.109), channel_id=1, source_target_pairs={{0,8},{8,16},{16,24},{24,32},{32,40},{40,48},{48,56},{56,64},{64,7... | collective-permute-start | bytes 196616 | tf_op jit(solution)/shard_map/ppermute | solution.py:30
  151.7 9.5 %collective-permute-start.11 = (f32[1,1024,16]{1,2,0:T(8,128)S(1)}, f32[1,1024,16]{1,2,0:T(8,128)S(1)}, u32[]{:S(2)}, u32[]{:S(2)}) collective-permute-start(f32[1,1024,16]{1,2,0:T(8,128)S(1)} %bitcast.110), channel_id=1, source_target_pairs={{8,0},{16,8},{24,16},{32,24},{40,32},{48,40},{56,48},{64,56},{72,6... | collective-permute-start | bytes 196616 | tf_op jit(solution)/shard_map/ppermute | solution.py:32
